TPU v7x, 128 devices: a whole 4x4x4 slice. The times are simulated.
128 devices in a mesh: ctx: 64 (over z, y, x), ch: 2 (over core).
Axes of the slice: x: 4, y: 4, z: 4, core: 2. Of those that a mesh axis runs over, the one named last changes fastest.
Arguments:
- conv_input: bfloat16 [16384, 8192], P(('ctx', 'ch')), may hold values from -6 to 6
- gate_branch: bfloat16 [16384, 8192], P(('ctx', 'ch')), may hold values from -6 to 6
- out_grad: bfloat16 [16384, 8192], P(('ctx', 'ch')), may hold values from -6 to 6
- short_filter: bfloat16 [7, 8192], P(None, 'ch'), may hold values from -2 to 2
- medium_filter: bfloat16 [128, 512], P(None, 'ch'), may hold values from -0.5 to 0.5
- decay_rates: float32 [512, 16], P('ch'), may hold values from 1.2207031e-05 to 0.125
- residues: float32 [512, 16], P('ch'), may hold values from -0.45 to 0.45
- direct_term: float32 [8192], P('ch'), may hold values from -3 to 3
Outputs:
- input_grad: bfloat16 [16384, 8192], P(('ctx', 'ch'))
- gate_grad: bfloat16 [16384, 8192], P(('ctx', 'ch'))
All inputs are finite; a program needn't handle non-finite values.
Results may differ from a plain program's by a relative error of at most 0.015.
Values may be sent and summed in bfloat16 or wider, within the bound.
A program may use at most 192 MiB of HBM per device.

v0:
```python
import functools

import jax
import jax.numpy as jnp
from jax import lax
from jax.experimental import pallas as pl
from jax.experimental.pallas import tpu as pltpu
from jax.sharding import PartitionSpec as P

MESH = pl.DeviceIdType.MESH
F32 = jnp.float32
BF16 = jnp.bfloat16
L = 128
G = 8
SPLIT = 4
UNROLL = 4


def iota(shape, dim):
    return lax.broadcasted_iota(jnp.int32, shape, dim)


def matmul(a, b):
    return lax.dot_general(a, b, (((1,), (0,)), ((), ())), preferred_element_type=F32)


def column(row):
    return jnp.broadcast_to(row, (L, L)).T


def own_groups(block):
    shape = block.shape
    keep = (iota(shape, 0) // 16) == ((iota(shape, 1) % L) // 16)
    return jnp.sum(jnp.where(keep, block, 0.0).reshape(G, 16, shape[1]), axis=0)


def spread_groups(states):
    shape = (L, states.shape[1])
    keep = (iota(shape, 0) // 16) == ((iota(shape, 1) % L) // 16)
    return jnp.where(keep, jnp.concatenate([states] * G, axis=0), 0.0)


def masked_stack(data):
    lanes = (iota((1, data.shape[1]), 1) % L) // 16
    return jnp.concatenate([data * (lanes == g).astype(F32).astype(BF16) for g in range(G)], axis=0)


def circulant(row):
    return pltpu.roll(jnp.broadcast_to(row, (L, L)), 0, 1, stride=1, stride_axis=0)


def kernel(
    x, gate, og, rate_in, weight_in, direct_in, short_in, medium_in, grad_out, gate_out,
    rate, weight, direct, short, medium, flipped, grad_y, taps, rate_lanes, sums, near, conv, adj, halo,
    buf_c, send_x, buf_x, send_y, buf_y, send_z, buf_z, push_y, buf_w, push_x, buf_r, push_c, states,
    head, head_next, tail, rows, ends,
    sem_p, sem_l, sem_n, sem_c, sem_x, sem_y, sem_z, sem_w, sem_r, sem_d, sem_h, sem_e,
):
    channels = x.shape[1]
    blocks = channels // L
    half, quarter, eighth = channels // 2, channels // 8, channels // 32
    ctx, c = lax.axis_index("ctx"), lax.axis_index("ch")
    px, py, pz = ctx % 4, (ctx // 4) % 4, ctx // 16
    me = ctx * 2 + c
    before_me, after_me = (me + 127) % 128, (me + 1) % 128
    last = me == 127

    def at(z_, y_, x_):
        return (z_ * 16 + y_ * 4 + x_, c)

    partner = (ctx, 1 - c)
    previous = (before_me // 2, before_me % 2)
    following = (after_me // 2, after_me % 2)
    mates_x = [at(pz, py, (px + d) % 4) for d in (1, 2, 3)]
    mates_y = [at(pz, (py + d) % 4, px) for d in (1, 2, 3)]
    mates_z = [at((pz + d) % 4, py, px) for d in (1, 2, 3)]
    barrier = pltpu.get_barrier_semaphore()
    for mate in [partner, following] + mates_x + mates_y + mates_z:
        pl.semaphore_signal(barrier, inc=1, device_id=mate, device_id_type=MESH)
    pl.semaphore_wait(barrier, 11)

    def push(src, dst, sem, k, mate):
        copy = pltpu.make_async_remote_copy(
            src, dst, sem.at[0, k], sem.at[1, k], device_id=mate, device_id_type=MESH
        )
        copy.start()
        return copy

    def lanes_of(start, size):
        return pl.ds(pl.multiple_of(start, L), size)

    copies = []
    for k, (own, full) in enumerate(
        [(rate_in, rate), (weight_in, weight), (direct_in, direct), (medium_in, medium)]
    ):
        count = own.shape[0]
        place = full.at[pl.ds(pl.multiple_of(c * count, 8), count), :]
        copies.append(push(own, place, sem_p, k, partner))
        here = pltpu.make_async_copy(own, place, sem_l.at[k])
        here.start()
        copies.append(here)
    mine, theirs = lanes_of(c * half, half), lanes_of((1 - c) * half, half)
    copies.append(push(short_in, short.at[:, mine], sem_p, 4, partner))
    here = pltpu.make_async_copy(short_in, short.at[:, mine], sem_l.at[4])
    here.start()
    copies.append(here)
    for copy in copies:
        copy.wait()

    lane, sub = iota((L, L), 1), iota((L, L), 0)
    flip = (lane + sub == 127).astype(F32).astype(BF16)

    def over_blocks(body, start, stop):
        def step(i, _):
            for u in range(UNROLL):
                body(i * UNROLL + u, u)
            return 0

        lax.fori_loop(start // UNROLL, stop // UNROLL, step, 0)

    def block_sums(b, u):
        cols = lanes_of(b * L, L)
        rate_col, weight_col = column(rate[pl.ds(b, 1), :]), column(weight[pl.ds(b, 1), :])
        decay = jnp.exp(-rate_col * lane.astype(F32))
        taps[pl.ds(pl.multiple_of(b * G, G), G), :] = jnp.sum((weight_col * decay).reshape(G, 16, L), axis=1)
        y = (og[:, cols].astype(F32) * gate[:, cols].astype(F32)).astype(BF16)
        back = matmul(flip, x[:, cols]).astype(BF16)
        grad_y[:, cols] = y
        flipped[:, cols] = back
        both = own_groups(matmul(decay.astype(BF16), jnp.concatenate([back, y], axis=1)))
        sums[0, :, cols] = both[:, :L].astype(BF16)
        sums[1, :, cols] = both[:, L:].astype(BF16)
        rate_lanes[:, cols] = own_groups(rate_col)

    def local_products(b, u):
        cols = lanes_of(b * L, L)
        k = taps[pl.ds(pl.multiple_of(b * G, G), G), :]
        table = [jnp.where(lane >= sub, circulant(k[g : g + 1, :]), 0.0).astype(BF16) for g in range(G)]
        y = grad_y[:, cols]
        data = jnp.concatenate([flipped[:, cols], y], axis=1)
        both = matmul(jnp.concatenate(table, axis=1), masked_stack(data))
        conv[:, cols] = both[:, :L].astype(BF16)
        adj[:, cols] = (both[:, L:] + direct[pl.ds(b, 1), :] * y.astype(F32)).astype(BF16)

    halo_copies = []

    def local_piece(k):
        size = blocks // SPLIT
        over_blocks(local_products, k * size, (k + 1) * size)
        cols = slice(k * size * L, (k + 1) * size * L)
        halo_copies.append(push(adj.at[:, cols], halo.at[:, cols], sem_h, k, previous))

    over_blocks(block_sums, 0, blocks)
    near_copy = push(sums.at[1], near, sem_n, 0, previous)
    fore_copy = push(sums.at[0, :, theirs], buf_c.at[0], sem_c, 0, partner)
    local_piece(0)
    near_copy.wait()

    near[...] = jnp.where(last, 0.0, near[...].astype(F32)).astype(BF16)
    back_copy = push(near.at[:, theirs], buf_c.at[1], sem_c, 1, partner)
    step = jnp.exp(-rate_lanes[:, mine] * 128.0)

    def ordered(own, other):
        return jnp.where(c == 0, own, other), jnp.where(c == 0, other, own)

    fore_copy.wait()
    first_a, second_a = ordered(sums[0, :, mine].astype(F32), buf_c[0].astype(F32))
    send_x[0] = (second_a + step * first_a).astype(BF16)
    back_copy.wait()
    first_b, second_b = ordered(near[:, mine].astype(F32), buf_c[1].astype(F32))
    send_x[1] = (first_b + step * second_b).astype(BF16)

    def power(rate_, span, count):
        return jnp.exp(-rate_ * (float(span) * jnp.maximum(count, 0).astype(F32)))

    def total(buf, span, rate_):
        p1 = jnp.exp(-rate_ * float(span))
        sum_a, sum_b = buf[0, 0].astype(F32), buf[3, 1].astype(F32)
        for j in (1, 2, 3):
            sum_a = sum_a * p1 + buf[j, 0].astype(F32)
            sum_b = sum_b * p1 + buf[3 - j, 1].astype(F32)
        return sum_a, sum_b

    def exclusive(buf, span, place, rate_, before, after):
        sum_a = before * power(rate_, span, place)
        sum_b = after * power(rate_, span, 3 - place)
        for j in range(4):
            sum_a += (j < place).astype(F32) * power(rate_, span, place - 1 - j) * buf[j, 0].astype(F32)
            sum_b += (j > place).astype(F32) * power(rate_, span, j - 1 - place) * buf[j, 1].astype(F32)
        return sum_a, sum_b

    def put(ref, pair):
        ref[0], ref[1] = pair[0].astype(BF16), pair[1].astype(BF16)

    copies = []
    for k, d in enumerate((1, 2, 3)):
        piece = send_x.at[:, :, lanes_of(((px + d) % 4) * quarter, quarter)]
        copies.append(push(piece, buf_x.at[px], sem_x, k, mates_x[k]))
    buf_x[px] = send_x[:, :, lanes_of(px * quarter, quarter)]
    rate_x = rate_lanes[:, lanes_of(c * half + px * quarter, quarter)]
    rate_y = rate_lanes[:, lanes_of(c * half + px * quarter + py * eighth, eighth)]
    local_piece(1)
    for copy in copies:
        copy.wait()
    put(send_y, total(buf_x, 256, rate_x))
    copies = []
    for k, d in enumerate((1, 2, 3)):
        piece = send_y.at[:, :, lanes_of(((py + d) % 4) * eighth, eighth)]
        copies.append(push(piece, buf_y.at[py], sem_y, k, mates_y[k]))
    buf_y[py] = send_y[:, :, lanes_of(py * eighth, eighth)]
    local_piece(2)
    for copy in copies:
        copy.wait()
    put(send_z, total(buf_y, 1024, rate_y))
    copies = [push(send_z, buf_z.at[pz], sem_z, k, mates_z[k]) for k in range(3)]
    buf_z[pz] = send_z[...]
    local_piece(3)
    for copy in copies:
        copy.wait()
    zero = jnp.zeros_like(rate_y)
    before, after = exclusive(buf_z, 4096, pz, rate_y, zero, zero)
    copies = []
    for k, d in enumerate((1, 2, 3)):
        put(push_y.at[k], exclusive(buf_y, 1024, (py + d) % 4, rate_y, before, after))
        copies.append(push(push_y.at[k], buf_w.at[py], sem_w, k, mates_y[k]))
    put(buf_w.at[py], exclusive(buf_y, 1024, py, rate_y, before, after))
    for copy in copies:
        copy.wait()
    before = jnp.concatenate([buf_w[j, 0] for j in range(4)], axis=1).astype(F32)
    after = jnp.concatenate([buf_w[j, 1] for j in range(4)], axis=1).astype(F32)
    copies = []
    for k, d in enumerate((1, 2, 3)):
        put(push_x.at[k], exclusive(buf_x, 256, (px + d) % 4, rate_x, before, after))
        copies.append(push(push_x.at[k], buf_r.at[px], sem_r, k, mates_x[k]))
    put(buf_r.at[px], exclusive(buf_x, 256, px, rate_x, before, after))
    for copy in copies:
        copy.wait()
    for j in range(4):
        lanes = pl.ds(j * quarter, quarter)
        part = slice(j * quarter, (j + 1) * quarter)
        early_a, late_b = buf_r[j, 0].astype(F32), buf_r[j, 1].astype(F32)
        late_a = first_a[:, part] + step[:, part] * early_a
        early_b = second_b[:, part] + step[:, part] * late_b
        push_c[0, :, lanes] = jnp.where(c == 0, late_a, early_a).astype(BF16)
        push_c[1, :, lanes] = jnp.where(c == 0, late_b, early_b).astype(BF16)
        keep = lanes_of(c * half + j * quarter, quarter)
        states[0, :, keep] = jnp.where(c == 0, early_a, late_a).astype(BF16)
        states[1, :, keep] = jnp.where(c == 0, early_b, late_b).astype(BF16)
    push(push_c, states.at[:, :, mine], sem_d, 0, partner).wait()
    for copy in halo_copies:
        copy.wait()

    for u in range(UNROLL):
        rows[u, L : L + 8, :] = jnp.zeros((8, L), F32)

    def adjoint_filters(b, u):
        cols = lanes_of(b * L, L)
        into = (weight[pl.ds(b, 1), :] * jnp.exp(-rate[pl.ds(b, 1), :] * (L - sub).astype(F32))).astype(BF16)
        far = states[1, :, cols].astype(F32)
        close = near[:, cols].astype(F32) + jnp.exp(-rate_lanes[:, cols] * 128.0) * far
        entering = spread_groups(jnp.concatenate([close, far], axis=1)).astype(BF16)
        beyond = jnp.where(last, 0.0, halo[:, cols].astype(F32))
        inside = jnp.concatenate([adj[:, cols].astype(F32), beyond], axis=1)
        grad_b = (inside + matmul(into, entering)).astype(BF16)
        m = medium[pl.ds(pl.multiple_of(b * G, G), G), :]
        now, then = [], []
        for g in range(G):
            table = circulant(m[g : g + 1, :])
            now.append(jnp.where(lane >= sub, table, 0.0).astype(BF16))
            then.append(jnp.where(lane < sub, table, 0.0).astype(BF16))
        tables = jnp.concatenate([jnp.concatenate(now, axis=1), jnp.concatenate(then, axis=1)], axis=0)
        both = matmul(tables, masked_stack(grad_b))
        grad_a = (both[:L, :L] + both[L:, L:]).astype(BF16)
        rows[u, 0:L, :] = grad_a.astype(F32)
        head[:, cols] = rows[u, 0:8, :]
        tail[:, cols] = rows[u, 112:128, :]
        taps_s = short[:, cols]
        sum_k = taps_s[0:1, :] * rows[u, 0:L, :]
        for k in range(1, 7):
            sum_k += taps_s[k : k + 1, :] * rows[u, k : k + L, :]
        grad_out[:, cols] = sum_k.astype(BF16)

    over_blocks(adjoint_filters, 0, blocks)
    head_copy = push(head, head_next, sem_e, 0, previous)

    def gate_gradient(b, u):
        cols = lanes_of(b * L, L)
        into = (weight[pl.ds(b, 1), :] * jnp.exp(-rate[pl.ds(b, 1), :] * (sub + 1).astype(F32))).astype(BF16)
        entering = spread_groups(states[0, :, cols].astype(F32)).astype(BF16)
        full = matmul(jnp.concatenate([flip, into], axis=1), jnp.concatenate([conv[:, cols], entering], axis=0))
        full = (full + direct[pl.ds(b, 1), :] * x[:, cols].astype(F32)).astype(BF16)
        gate_out[:, cols] = (og[:, cols].astype(F32) * full.astype(F32)).astype(BF16)

    over_blocks(gate_gradient, 0, blocks)
    head_copy.wait()

    def last_rows(b, u):
        cols = lanes_of(b * L, L)
        ends[u, 0:16, :] = tail[:, cols]
        ends[u, 16:24, :] = jnp.where(last, 0.0, head_next[:, cols])
        taps_s = short[:, cols]
        sum_k = taps_s[0:1, :] * ends[u, 0:16, :]
        for k in range(1, 7):
            sum_k += taps_s[k : k + 1, :] * ends[u, k : k + 16, :]
        grad_out[112:128, cols] = sum_k.astype(BF16)

    over_blocks(last_rows, 0, blocks)


def on_device(x, gate, og, short_filter, medium_filter, decay_rates, residues, direct_term):
    channels = x.shape[1]
    groups = channels // 16
    rows = decay_rates.shape[0] // G
    half, quarter, eighth = channels // 2, channels // 8, channels // 32
    wide = pltpu.VMEM((L, channels), BF16)
    vmem, dma = pltpu.VMEM, pltpu.SemaphoreType.DMA
    return pl.pallas_call(
        kernel,
        out_shape=(jax.ShapeDtypeStruct(x.shape, BF16),) * 2,
        in_specs=[pl.BlockSpec(memory_space=pltpu.VMEM)] * 8,
        out_specs=(pl.BlockSpec(memory_space=pltpu.VMEM),) * 2,
        scratch_shapes=[
            vmem((2 * rows, L), F32),
            vmem((2 * rows, L), F32),
            vmem((2 * rows, L), F32),
            vmem((8, channels), F32),
            vmem((groups, L), F32),
            wide,
            wide,
            vmem((groups, L), F32),
            vmem((16, channels), F32),
            vmem((2, 16, channels), BF16),
            vmem((16, channels), BF16),
            wide,
            wide,
            wide,
            vmem((2, 16, half), BF16),
            vmem((2, 16, half), BF16),
            vmem((4, 2, 16, quarter), BF16),
            vmem((2, 16, quarter), BF16),
            vmem((4, 2, 16, eighth), BF16),
            vmem((2, 16, eighth), BF16),
            vmem((4, 2, 16, eighth), BF16),
            vmem((3, 2, 16, eighth), BF16),
            vmem((4, 2, 16, eighth), BF16),
            vmem((3, 2, 16, quarter), BF16),
            vmem((4, 2, 16, quarter), BF16),
            vmem((2, 16, half), BF16),
            vmem((2, 16, channels), BF16),
            vmem((8, channels), F32),
            vmem((8, channels), F32),
            vmem((16, channels), F32),
            vmem((UNROLL, L + 8, L), F32),
            vmem((UNROLL, 24, L), F32),
            dma((2, 5)), dma((5,)), dma((2, 1)), dma((2, 2)), dma((2, 3)), dma((2, 3)), dma((2, 3)),
            dma((2, 3)), dma((2, 3)), dma((2, 1)), dma((2, SPLIT)), dma((2, 1)),
        ],
        compiler_params=pltpu.CompilerParams(
            collective_id=0, has_side_effects=True, vmem_limit_bytes=58 * 2**20
        ),
    )(
        x,
        gate,
        og,
        decay_rates.reshape(rows, L),
        residues.reshape(rows, L),
        direct_term.reshape(rows, L),
        jnp.pad(short_filter.astype(F32), ((0, 1), (0, 0))),
        medium_filter.astype(F32).T,
    )


def solution(mesh):
    placed = (
        P(("ctx", "ch"), None),
        P(("ctx", "ch"), None),
        P(("ctx", "ch"), None),
        P(None, "ch"),
        P(None, "ch"),
        P("ch", None),
        P("ch", None),
        P("ch"),
    )
    return jax.shard_map(
        on_device,
        mesh=mesh,
        in_specs=placed,
        out_specs=(P(("ctx", "ch"), None), P(("ctx", "ch"), None)),
        check_vma=False,
    )
```

profile of v0, /device:TPU:31, one launch (start us, length us, event | category | flops | bytes accessed | tf_op | source)
XLA Modules:
  0.0 101.9 jit_solution(11769067713533522162)
XLA Ops:
  0.6 0.9 copy.15
  1.6 0.7 convert_bitcast_fusion.medium_in
  2.3 1.5 %pad_convert_fusion.short_in = f32[8,4096]{1,0:T(8,128)} fusion(bf16[7,4096]{1,0:T(8,128)(2,1)} %param.11), kind=kLoop, calls=%fused_computation.1 | loop fusion | flops 32768 | bytes 188416 | tf_op jit(solution)/shard_map/jit(_pad)/pad | solution.py:368
  3.8 0.8 copy.13
  4.6 0.7 reshape.13.rate_in
  5.3 0.8 copy.14
  6.1 0.7 reshape.14.weight_in
  6.8 90.5 %shard_map.95 = (bf16[128,8192]{1,0:T(8,128)(2,1)}, bf16[128,8192]{1,0:T(8,128)(2,1)}) custom-call(bf16[128,8192]{1,0:T(8,128)(2,1)} %x.3, bf16[128,8192]{1,0:T(8,128)(2,1)} %gate.1, bf16[128,8192]{1,0:T(8,128)(2,1)} %og.1, f32[32,128]{1,0:T(8,128)} %reshape.13.rate_in, f32[32,128]{1,0:T(8,128)} %reshape.14.weight_in, f32[32,128]{1,0:T(8,128)} %bitcast.3, ...), custom_call_target="tpu_custom_call" | custom-call | tf_op jit(solution)/shard_map/pallas_call | solution.py:317
  97.4 0.0 copy-start
  97.4 3.2 %copy.18 = bf16[128,8192]{1,0:T(8,128)(2,1)} copy(bf16[128,8192]{1,0:T(8,128)(2,1)} %get-tuple-element.4) | data formatting | bytes 4194304
  100.6 0.0 copy-done
  100.6 1.3 %copy.19 = bf16[128,8192]{1,0:T(8,128)(2,1)} copy(bf16[128,8192]{1,0:T(8,128)(2,1)S(1)} %copy-done) | data formatting | bytes 4194304
Async XLA Ops:
  97.4 3.3 %copy-start = (bf16[128,8192]{1,0:T(8,128)(2,1)S(1)}, bf16[128,8192]{1,0:T(8,128)(2,1)}, u32[]{:S(2)}) copy-start(bf16[128,8192]{1,0:T(8,128)(2,1)} %get-tuple-element.5) | copy-start | bytes 6291460
where the time goes:
time: 102 us
  Pallas kernels  90.5 us (89%)
  local copies, waits for them, and re-layouts  8.56 us (8%)
  other arithmetic  2.18 us (2%)
    pallas_call x1, Pallas kernels, on_device(): pl.pallas_call(kernel, out_shape=(jax.ShapeDtypeStruct(x.shape, BF16),) *...  90.5 us
    unnamed x7, local copies, waits for them, and re-layouts  7.15 us

commit v1 on v0

--- a/solution.py
+++ b/solution.py
@@ -12,7 +12,7 @@
 BF16 = jnp.bfloat16
 L = 128
 G = 8
-SPLIT = 4
+SPLIT = 8
 UNROLL = 4
 
 
@@ -50,14 +50,16 @@
 
 
 def kernel(
-    x, gate, og, rate_in, weight_in, direct_in, short_in, medium_in, grad_out, gate_out,
+    x_in, gate_in, og_in, rate_in, weight_in, direct_in, short_in, medium_in, grad_done, gate_done,
+    x, gate, og, grad_out, gate_out, rate_by_group, weight_by_group, medium_raw, circ,
     rate, weight, direct, short, medium, flipped, grad_y, taps, rate_lanes, sums, near, conv, adj, halo,
     buf_c, send_x, buf_x, send_y, buf_y, send_z, buf_z, push_y, buf_w, push_x, buf_r, push_c, states,
     head, head_next, tail, rows, ends,
-    sem_p, sem_l, sem_n, sem_c, sem_x, sem_y, sem_z, sem_w, sem_r, sem_d, sem_h, sem_e,
+    sem_i, sem_o, sem_p, sem_l, sem_n, sem_c, sem_x, sem_y, sem_z, sem_w, sem_r, sem_d, sem_h, sem_e,
 ):
-    channels = x.shape[1]
+    channels = x_in.shape[1]
     blocks = channels // L
+    wide = channels // SPLIT
     half, quarter, eighth = channels // 2, channels // 8, channels // 32
     ctx, c = lax.axis_index("ctx"), lax.axis_index("ch")
     px, py, pz = ctx % 4, (ctx // 4) % 4, ctx // 16
@@ -74,6 +76,10 @@
     mates_x = [at(pz, py, (px + d) % 4) for d in (1, 2, 3)]
     mates_y = [at(pz, (py + d) % 4, px) for d in (1, 2, 3)]
     mates_z = [at((pz + d) % 4, py, px) for d in (1, 2, 3)]
+    loads = []
+    for k, (src, dst) in enumerate([(x_in, x), (gate_in, gate), (og_in, og)]):
+        loads.append(pltpu.make_async_copy(src, dst, sem_i.at[k]))
+        loads[-1].start()
     barrier = pltpu.get_barrier_semaphore()
     for mate in [partner, following] + mates_x + mates_y + mates_z:
         pl.semaphore_signal(barrier, inc=1, device_id=mate, device_id_type=MESH)
@@ -89,38 +95,48 @@
     def lanes_of(start, size):
         return pl.ds(pl.multiple_of(start, L), size)
 
-    copies = []
-    for k, (own, full) in enumerate(
-        [(rate_in, rate), (weight_in, weight), (direct_in, direct), (medium_in, medium)]
-    ):
-        count = own.shape[0]
-        place = full.at[pl.ds(pl.multiple_of(c * count, 8), count), :]
-        copies.append(push(own, place, sem_p, k, partner))
-        here = pltpu.make_async_copy(own, place, sem_l.at[k])
-        here.start()
-        copies.append(here)
     mine, theirs = lanes_of(c * half, half), lanes_of((1 - c) * half, half)
-    copies.append(push(short_in, short.at[:, mine], sem_p, 4, partner))
-    here = pltpu.make_async_copy(short_in, short.at[:, mine], sem_l.at[4])
-    here.start()
-    copies.append(here)
-    for copy in copies:
+    count = rate_in.shape[1]
+    groups_mine = lanes_of(c * count, count)
+    places = [
+        (rate_in, rate_by_group.at[:, groups_mine]),
+        (weight_in, weight_by_group.at[:, groups_mine]),
+        (medium_in, medium_raw.at[:, groups_mine]),
+        (direct_in, direct.at[pl.ds(pl.multiple_of(c * direct_in.shape[0], 8), direct_in.shape[0]), :]),
+        (short_in, short.at[:, mine]),
+    ]
+    gathers, here = [], []
+    for k, (own, place) in enumerate(places):
+        gathers.append(push(own, place, sem_p, k, partner))
+        here.append(pltpu.make_async_copy(own, place, sem_l.at[k]))
+        here[-1].start()
+    for copy in here + loads:
         copy.wait()
 
     lane, sub = iota((L, L), 1), iota((L, L), 0)
     flip = (lane + sub == 127).astype(F32).astype(BF16)
 
-    def over_blocks(body, start, stop):
+    def over_blocks(body, start, size):
         def step(i, _):
             for u in range(UNROLL):
-                body(i * UNROLL + u, u)
+                body(start + i * UNROLL + u, u)
             return 0
 
-        lax.fori_loop(start // UNROLL, stop // UNROLL, step, 0)
+        lax.fori_loop(0, size // UNROLL, step, 0)
 
     def block_sums(b, u):
         cols = lanes_of(b * L, L)
-        rate_col, weight_col = column(rate[pl.ds(b, 1), :]), column(weight[pl.ds(b, 1), :])
+        tile = lanes_of((b // 16) * L, L)
+        pick = (b % 16) * G + iota((16, L), 1) // 16
+        diagonal = iota((16, L), 0) == iota((16, L), 1) % 16
+        rate_here = jnp.take_along_axis(rate_by_group[:, tile], pick, axis=1)
+        weight_here = jnp.take_along_axis(weight_by_group[:, tile], pick, axis=1)
+        rate_row = jnp.sum(jnp.where(diagonal, rate_here, 0.0), axis=0, keepdims=True)
+        weight_row = jnp.sum(jnp.where(diagonal, weight_here, 0.0), axis=0, keepdims=True)
+        rate_lanes[:, cols] = rate_here
+        rate[pl.ds(b, 1), :] = rate_row
+        weight[pl.ds(b, 1), :] = weight_row
+        rate_col, weight_col = column(rate_row), column(weight_row)
         decay = jnp.exp(-rate_col * lane.astype(F32))
         taps[pl.ds(pl.multiple_of(b * G, G), G), :] = jnp.sum((weight_col * decay).reshape(G, 16, L), axis=1)
         y = (og[:, cols].astype(F32) * gate[:, cols].astype(F32)).astype(BF16)
@@ -130,7 +146,6 @@
         both = own_groups(matmul(decay.astype(BF16), jnp.concatenate([back, y], axis=1)))
         sums[0, :, cols] = both[:, :L].astype(BF16)
         sums[1, :, cols] = both[:, L:].astype(BF16)
-        rate_lanes[:, cols] = own_groups(rate_col)
 
     def local_products(b, u):
         cols = lanes_of(b * L, L)
@@ -142,18 +157,31 @@
         conv[:, cols] = both[:, :L].astype(BF16)
         adj[:, cols] = (both[:, L:] + direct[pl.ds(b, 1), :] * y.astype(F32)).astype(BF16)
 
+    def medium_tables(b, u):
+        m = medium[pl.ds(pl.multiple_of(b * G, G), G), :]
+        for g in range(G):
+            circ[b, :, g * L : g * L + L] = circulant(m[g : g + 1, :]).astype(BF16)
+
+    size = blocks // SPLIT
     halo_copies = []
 
-    def local_piece(k):
-        size = blocks // SPLIT
-        over_blocks(local_products, k * size, (k + 1) * size)
-        cols = slice(k * size * L, (k + 1) * size * L)
-        halo_copies.append(push(adj.at[:, cols], halo.at[:, cols], sem_h, k, previous))
-
-    over_blocks(block_sums, 0, blocks)
+    def local_pieces(first, stop):
+        over_blocks(local_products, first * size, (stop - first) * size)
+
+    def push_halo(first, stop):
+        for k in range(first, stop):
+            cols = slice(k * wide, (k + 1) * wide)
+            halo_copies.append(push(adj.at[:, cols], halo.at[:, cols], sem_h, k, previous))
+
+    over_blocks(block_sums, c * (blocks // 2), blocks // 2)
+    for copy in gathers:
+        copy.wait()
+    over_blocks(block_sums, (1 - c) * (blocks // 2), blocks // 2)
     near_copy = push(sums.at[1], near, sem_n, 0, previous)
     fore_copy = push(sums.at[0, :, theirs], buf_c.at[0], sem_c, 0, partner)
-    local_piece(0)
+    for k in range(medium.shape[0] // L):
+        medium[k * L : k * L + L, :] = medium_raw[:, k * L : k * L + L].astype(F32).T
+    local_pieces(0, 1)
     near_copy.wait()
 
     near[...] = jnp.where(last, 0.0, near[...].astype(F32)).astype(BF16)
@@ -199,7 +227,7 @@
     buf_x[px] = send_x[:, :, lanes_of(px * quarter, quarter)]
     rate_x = rate_lanes[:, lanes_of(c * half + px * quarter, quarter)]
     rate_y = rate_lanes[:, lanes_of(c * half + px * quarter + py * eighth, eighth)]
-    local_piece(1)
+    local_pieces(1, 4)
     for copy in copies:
         copy.wait()
     put(send_y, total(buf_x, 256, rate_x))
@@ -208,13 +236,14 @@
         piece = send_y.at[:, :, lanes_of(((py + d) % 4) * eighth, eighth)]
         copies.append(push(piece, buf_y.at[py], sem_y, k, mates_y[k]))
     buf_y[py] = send_y[:, :, lanes_of(py * eighth, eighth)]
-    local_piece(2)
+    push_halo(0, 3)
+    local_pieces(4, 6)
     for copy in copies:
         copy.wait()
     put(send_z, total(buf_y, 1024, rate_y))
     copies = [push(send_z, buf_z.at[pz], sem_z, k, mates_z[k]) for k in range(3)]
     buf_z[pz] = send_z[...]
-    local_piece(3)
+    local_pieces(6, 8)
     for copy in copies:
         copy.wait()
     zero = jnp.zeros_like(rate_y)
@@ -224,6 +253,7 @@
         put(push_y.at[k], exclusive(buf_y, 1024, (py + d) % 4, rate_y, before, after))
         copies.append(push(push_y.at[k], buf_w.at[py], sem_w, k, mates_y[k]))
     put(buf_w.at[py], exclusive(buf_y, 1024, py, rate_y, before, after))
+    over_blocks(medium_tables, 0, blocks // 2)
     for copy in copies:
         copy.wait()
     before = jnp.concatenate([buf_w[j, 0] for j in range(4)], axis=1).astype(F32)
@@ -233,8 +263,10 @@
         put(push_x.at[k], exclusive(buf_x, 256, (px + d) % 4, rate_x, before, after))
         copies.append(push(push_x.at[k], buf_r.at[px], sem_r, k, mates_x[k]))
     put(buf_r.at[px], exclusive(buf_x, 256, px, rate_x, before, after))
+    over_blocks(medium_tables, blocks // 2, blocks // 2)
     for copy in copies:
         copy.wait()
+    push_halo(3, SPLIT)
     for j in range(4):
         lanes = pl.ds(j * quarter, quarter)
         part = slice(j * quarter, (j + 1) * quarter)
@@ -247,11 +279,12 @@
         states[0, :, keep] = jnp.where(c == 0, early_a, late_a).astype(BF16)
         states[1, :, keep] = jnp.where(c == 0, early_b, late_b).astype(BF16)
     push(push_c, states.at[:, :, mine], sem_d, 0, partner).wait()
-    for copy in halo_copies:
-        copy.wait()
 
     for u in range(UNROLL):
         rows[u, L : L + 8, :] = jnp.zeros((8, L), F32)
+
+    upper = jnp.concatenate([(lane >= sub).astype(F32).astype(BF16)] * G, axis=1)
+    lower = jnp.concatenate([(lane < sub).astype(F32).astype(BF16)] * G, axis=1)
 
     def adjoint_filters(b, u):
         cols = lanes_of(b * L, L)
@@ -262,26 +295,18 @@
         beyond = jnp.where(last, 0.0, halo[:, cols].astype(F32))
         inside = jnp.concatenate([adj[:, cols].astype(F32), beyond], axis=1)
         grad_b = (inside + matmul(into, entering)).astype(BF16)
-        m = medium[pl.ds(pl.multiple_of(b * G, G), G), :]
-        now, then = [], []
-        for g in range(G):
-            table = circulant(m[g : g + 1, :])
-            now.append(jnp.where(lane >= sub, table, 0.0).astype(BF16))
-            then.append(jnp.where(lane < sub, table, 0.0).astype(BF16))
-        tables = jnp.concatenate([jnp.concatenate(now, axis=1), jnp.concatenate(then, axis=1)], axis=0)
+        table = circ[b]
+        tables = jnp.concatenate([table * upper, table * lower], axis=0)
         both = matmul(tables, masked_stack(grad_b))
         grad_a = (both[:L, :L] + both[L:, L:]).astype(BF16)
         rows[u, 0:L, :] = grad_a.astype(F32)
-        head[:, cols] = rows[u, 0:8, :]
+        head[:, cols] = rows[u, 0:8, :].astype(BF16)
         tail[:, cols] = rows[u, 112:128, :]
-        taps_s = short[:, cols]
+        taps_s = short[:, cols].astype(F32)
         sum_k = taps_s[0:1, :] * rows[u, 0:L, :]
         for k in range(1, 7):
             sum_k += taps_s[k : k + 1, :] * rows[u, k : k + L, :]
         grad_out[:, cols] = sum_k.astype(BF16)
-
-    over_blocks(adjoint_filters, 0, blocks)
-    head_copy = push(head, head_next, sem_e, 0, previous)
 
     def gate_gradient(b, u):
         cols = lanes_of(b * L, L)
@@ -291,20 +316,35 @@
         full = (full + direct[pl.ds(b, 1), :] * x[:, cols].astype(F32)).astype(BF16)
         gate_out[:, cols] = (og[:, cols].astype(F32) * full.astype(F32)).astype(BF16)
 
-    over_blocks(gate_gradient, 0, blocks)
-    head_copy.wait()
+    head_copies, stores = [], []
+    for k in range(SPLIT):
+        cols = slice(k * wide, (k + 1) * wide)
+        halo_copies[k].wait()
+        over_blocks(adjoint_filters, k * size, size)
+        head_copies.append(push(head.at[:, cols], head_next.at[:, cols], sem_e, k, previous))
+        over_blocks(gate_gradient, k * size, size)
+        stores.append(pltpu.make_async_copy(gate_out.at[:, cols], gate_done.at[:, cols], sem_o.at[0, k]))
+        stores.append(pltpu.make_async_copy(grad_out.at[0:112, cols], grad_done.at[0:112, cols], sem_o.at[1, k]))
+        for copy in stores[-2:]:
+            copy.start()
+    for copy in head_copies:
+        copy.wait()
 
     def last_rows(b, u):
         cols = lanes_of(b * L, L)
         ends[u, 0:16, :] = tail[:, cols]
-        ends[u, 16:24, :] = jnp.where(last, 0.0, head_next[:, cols])
-        taps_s = short[:, cols]
+        ends[u, 16:24, :] = jnp.where(last, 0.0, head_next[:, cols].astype(F32))
+        taps_s = short[:, cols].astype(F32)
         sum_k = taps_s[0:1, :] * ends[u, 0:16, :]
         for k in range(1, 7):
             sum_k += taps_s[k : k + 1, :] * ends[u, k : k + 16, :]
         grad_out[112:128, cols] = sum_k.astype(BF16)
 
     over_blocks(last_rows, 0, blocks)
+    stores.append(pltpu.make_async_copy(grad_out.at[112:128, :], grad_done.at[112:128, :], sem_o.at[2, 0]))
+    stores[-1].start()
+    for copy in stores:
+        copy.wait()
 
 
 def on_device(x, gate, og, short_filter, medium_filter, decay_rates, residues, direct_term):
@@ -317,13 +357,18 @@
     return pl.pallas_call(
         kernel,
         out_shape=(jax.ShapeDtypeStruct(x.shape, BF16),) * 2,
-        in_specs=[pl.BlockSpec(memory_space=pltpu.VMEM)] * 8,
-        out_specs=(pl.BlockSpec(memory_space=pltpu.VMEM),) * 2,
+        in_specs=[pl.BlockSpec(memory_space=pl.ANY)] * 3 + [pl.BlockSpec(memory_space=pltpu.VMEM)] * 5,
+        out_specs=(pl.BlockSpec(memory_space=pl.ANY),) * 2,
         scratch_shapes=[
+            wide, wide, wide, wide, wide,
+            vmem((16, groups), F32),
+            vmem((16, groups), F32),
+            vmem((L, groups), BF16),
+            vmem((channels // L, L, G * L), BF16),
             vmem((2 * rows, L), F32),
             vmem((2 * rows, L), F32),
             vmem((2 * rows, L), F32),
-            vmem((8, channels), F32),
+            vmem((7, channels), BF16),
             vmem((groups, L), F32),
             wide,
             wide,
@@ -347,13 +392,13 @@
             vmem((4, 2, 16, quarter), BF16),
             vmem((2, 16, half), BF16),
             vmem((2, 16, channels), BF16),
-            vmem((8, channels), F32),
-            vmem((8, channels), F32),
+            vmem((8, channels), BF16),
+            vmem((8, channels), BF16),
             vmem((16, channels), F32),
             vmem((UNROLL, L + 8, L), F32),
             vmem((UNROLL, 24, L), F32),
-            dma((2, 5)), dma((5,)), dma((2, 1)), dma((2, 2)), dma((2, 3)), dma((2, 3)), dma((2, 3)),
-            dma((2, 3)), dma((2, 3)), dma((2, 1)), dma((2, SPLIT)), dma((2, 1)),
+            dma((3,)), dma((3, SPLIT)), dma((2, 5)), dma((5,)), dma((2, 1)), dma((2, 2)), dma((2, 3)), dma((2, 3)), dma((2, 3)),
+            dma((2, 3)), dma((2, 3)), dma((2, 1)), dma((2, SPLIT)), dma((2, SPLIT)),
         ],
         compiler_params=pltpu.CompilerParams(
             collective_id=0, has_side_effects=True, vmem_limit_bytes=58 * 2**20
@@ -362,11 +407,11 @@
         x,
         gate,
         og,
-        decay_rates.reshape(rows, L),
-        residues.reshape(rows, L),
+        decay_rates.T,
+        residues.T,
         direct_term.reshape(rows, L),
-        jnp.pad(short_filter.astype(F32), ((0, 1), (0, 0))),
-        medium_filter.astype(F32).T,
+        short_filter,
+        medium_filter,
     )
 
 

time: 102 us -> 84.8 us (0.83)
  Pallas kernels: 90.5 us -> 79.5 us
  local copies, waits for them, and re-layouts: 8.56 us -> 4.57 us
  other arithmetic: 2.18 us -> 0 us
    pallas_call x1, Pallas kernels: 90.5 us -> 79.5 us  [on_device(): pl.pallas_call(kernel, out_shape=(jax.ShapeDtypeStruct(x.shape, BF16),) *...]
    unnamed x7 -> x4, local copies, waits for them, and re-layouts: 7.15 us -> 4.57 us
    pad x1 -> x0, other arithmetic: 1.5 us -> none  [on_device(): jnp.pad(short_filter.astype(F32), ((0, 1), (0, 0)))]
    reshape x2 -> x0, local copies, waits for them, and re-layouts: 1.42 us -> none  [the longest x1 0.72 us: on_device(): decay_rates.reshape(rows, L)]
where the time goes in v1:
time: 84.8 us; the launch traced here: 84.7 us
  Pallas kernels  79.5 us (94%)
  local copies, waits for them, and re-layouts  4.57 us (5%)
    pallas_call x1, Pallas kernels, on_device(): pl.pallas_call(kernel, out_shape=(jax.ShapeDtypeStruct(x.shape, BF16),) *...  79.5 us
    unnamed x4, local copies, waits for them, and re-layouts  4.57 us

profile of v1, /device:TPU:31, one launch (start us, length us, event | category | flops | bytes accessed | tf_op | source)
XLA Modules:
  0.0 84.7 jit_solution(1022757801504696465)
XLA Ops:
  0.6 79.5 %shard_map.95 = (bf16[128,8192]{1,0:T(8,128)(2,1)}, bf16[128,8192]{1,0:T(8,128)(2,1)}) custom-call(bf16[128,8192]{1,0:T(8,128)(2,1)} %x_in.1, bf16[128,8192]{1,0:T(8,128)(2,1)} %gate_in.1, bf16[128,8192]{1,0:T(8,128)(2,1)} %og_in.1, f32[16,256]{1,0:T(8,128)} %bitcast.3, f32[16,256]{1,0:T(8,128)} %bitcast.4, f32[32,128]{1,0:T(8,128)} %bitcast.5, ...), custom_call_target="tpu_custom_call" | custom-call | tf_op jit(solution)/shard_map/pallas_call | solution.py:357
  80.1 0.0 copy-start
  80.1 3.2 %copy.12 = bf16[128,8192]{1,0:T(8,128)(2,1)} copy(bf16[128,8192]{1,0:T(8,128)(2,1)} %get-tuple-element.4) | data formatting | bytes 4194304
  83.4 0.0 copy-done
  83.4 1.3 %copy.13 = bf16[128,8192]{1,0:T(8,128)(2,1)} copy(bf16[128,8192]{1,0:T(8,128)(2,1)S(1)} %copy-done) | data formatting | bytes 4194304
Async XLA Ops:
  80.1 3.3 %copy-start = (bf16[128,8192]{1,0:T(8,128)(2,1)S(1)}, bf16[128,8192]{1,0:T(8,128)(2,1)}, u32[]{:S(2)}) copy-start(bf16[128,8192]{1,0:T(8,128)(2,1)} %get-tuple-element.5) | copy-start | bytes 6291460

commit v2 on v1

--- a/solution.py
+++ b/solution.py
@@ -52,8 +52,8 @@
 def kernel(
     x_in, gate_in, og_in, rate_in, weight_in, direct_in, short_in, medium_in, grad_done, gate_done,
     x, gate, og, grad_out, gate_out, rate_by_group, weight_by_group, medium_raw, circ,
-    rate, weight, direct, short, medium, flipped, grad_y, taps, rate_lanes, sums, near, conv, adj, halo,
-    buf_c, send_x, buf_x, send_y, buf_y, send_z, buf_z, push_y, buf_w, push_x, buf_r, push_c, states,
+    rate, weight, direct, short, medium, grad_y, rate_lanes, sums, near, conv, adj, halo,
+    buf_c, send_x, buf_x, send_y, buf_y, send_z, buf_z, push_z, push_y, buf_w, push_x, buf_r, push_c, states,
     head, head_next, tail, rows, ends,
     sem_i, sem_o, sem_p, sem_l, sem_n, sem_c, sem_x, sem_y, sem_z, sem_w, sem_r, sem_d, sem_h, sem_e,
 ):
@@ -83,7 +83,6 @@
     barrier = pltpu.get_barrier_semaphore()
     for mate in [partner, following] + mates_x + mates_y + mates_z:
         pl.semaphore_signal(barrier, inc=1, device_id=mate, device_id_type=MESH)
-    pl.semaphore_wait(barrier, 11)
 
     def push(src, dst, sem, k, mate):
         copy = pltpu.make_async_remote_copy(
@@ -105,9 +104,8 @@
         (direct_in, direct.at[pl.ds(pl.multiple_of(c * direct_in.shape[0], 8), direct_in.shape[0]), :]),
         (short_in, short.at[:, mine]),
     ]
-    gathers, here = [], []
+    here = []
     for k, (own, place) in enumerate(places):
-        gathers.append(push(own, place, sem_p, k, partner))
         here.append(pltpu.make_async_copy(own, place, sem_l.at[k]))
         here[-1].start()
     for copy in here + loads:
@@ -136,23 +134,23 @@
         rate_lanes[:, cols] = rate_here
         rate[pl.ds(b, 1), :] = rate_row
         weight[pl.ds(b, 1), :] = weight_row
-        rate_col, weight_col = column(rate_row), column(weight_row)
-        decay = jnp.exp(-rate_col * lane.astype(F32))
-        taps[pl.ds(pl.multiple_of(b * G, G), G), :] = jnp.sum((weight_col * decay).reshape(G, 16, L), axis=1)
+        rate_col = column(rate_row)
+        ahead = jnp.exp(-rate_col * (127 - lane).astype(F32)).astype(BF16)
+        behind = jnp.exp(-rate_col * lane.astype(F32)).astype(BF16)
         y = (og[:, cols].astype(F32) * gate[:, cols].astype(F32)).astype(BF16)
-        back = matmul(flip, x[:, cols]).astype(BF16)
         grad_y[:, cols] = y
-        flipped[:, cols] = back
-        both = own_groups(matmul(decay.astype(BF16), jnp.concatenate([back, y], axis=1)))
-        sums[0, :, cols] = both[:, :L].astype(BF16)
-        sums[1, :, cols] = both[:, L:].astype(BF16)
+        both = matmul(jnp.concatenate([ahead, behind], axis=0), jnp.concatenate([x[:, cols], y], axis=1))
+        sums[0, :, cols] = own_groups(both[:L, :L]).astype(BF16)
+        sums[1, :, cols] = own_groups(both[L:, L:]).astype(BF16)
 
     def local_products(b, u):
         cols = lanes_of(b * L, L)
-        k = taps[pl.ds(pl.multiple_of(b * G, G), G), :]
+        decay = jnp.exp(-column(rate[pl.ds(b, 1), :]) * lane.astype(F32))
+        k = jnp.sum((column(weight[pl.ds(b, 1), :]) * decay).reshape(G, 16, L), axis=1)
+        back = matmul(flip, x[:, cols]).astype(BF16)
         table = [jnp.where(lane >= sub, circulant(k[g : g + 1, :]), 0.0).astype(BF16) for g in range(G)]
         y = grad_y[:, cols]
-        data = jnp.concatenate([flipped[:, cols], y], axis=1)
+        data = jnp.concatenate([back, y], axis=1)
         both = matmul(jnp.concatenate(table, axis=1), masked_stack(data))
         conv[:, cols] = both[:, :L].astype(BF16)
         adj[:, cols] = (both[:, L:] + direct[pl.ds(b, 1), :] * y.astype(F32)).astype(BF16)
@@ -165,41 +163,38 @@
     size = blocks // SPLIT
     halo_copies = []
 
+    def piece(k, core):
+        return (core * (SPLIT // 2) + k) % SPLIT
+
     def local_pieces(first, stop):
-        over_blocks(local_products, first * size, (stop - first) * size)
+        for k in range(first, stop):
+            over_blocks(local_products, piece(k, c) * size, size)
 
     def push_halo(first, stop):
         for k in range(first, stop):
-            cols = slice(k * wide, (k + 1) * wide)
+            cols = lanes_of(piece(k, c) * wide, wide)
             halo_copies.append(push(adj.at[:, cols], halo.at[:, cols], sem_h, k, previous))
 
     over_blocks(block_sums, c * (blocks // 2), blocks // 2)
+    pl.semaphore_wait(barrier, 11)
+    gathers = [push(own, place, sem_p, k, partner) for k, (own, place) in enumerate(places)]
+    local_pieces(0, 1)
     for copy in gathers:
         copy.wait()
     over_blocks(block_sums, (1 - c) * (blocks // 2), blocks // 2)
-    near_copy = push(sums.at[1], near, sem_n, 0, previous)
-    fore_copy = push(sums.at[0, :, theirs], buf_c.at[0], sem_c, 0, partner)
+    first_copy = push(sums.at[:, :, theirs], buf_c, sem_c, 0, partner)
     for k in range(medium.shape[0] // L):
         medium[k * L : k * L + L, :] = medium_raw[:, k * L : k * L + L].astype(F32).T
-    local_pieces(0, 1)
-    near_copy.wait()
-
-    near[...] = jnp.where(last, 0.0, near[...].astype(F32)).astype(BF16)
-    back_copy = push(near.at[:, theirs], buf_c.at[1], sem_c, 1, partner)
+    local_pieces(1, 2)
+
     step = jnp.exp(-rate_lanes[:, mine] * 128.0)
-
-    def ordered(own, other):
-        return jnp.where(c == 0, own, other), jnp.where(c == 0, other, own)
-
-    fore_copy.wait()
-    first_a, second_a = ordered(sums[0, :, mine].astype(F32), buf_c[0].astype(F32))
+    own = sums[:, :, mine].astype(F32)
+    first_copy.wait()
+    other = buf_c[...].astype(F32)
+    first_a, second_a = jnp.where(c == 0, own[0], other[0]), jnp.where(c == 0, other[0], own[0])
+    first_b, second_b = jnp.where(c == 0, own[1], other[1]), jnp.where(c == 0, other[1], own[1])
     send_x[0] = (second_a + step * first_a).astype(BF16)
-    back_copy.wait()
-    first_b, second_b = ordered(near[:, mine].astype(F32), buf_c[1].astype(F32))
     send_x[1] = (first_b + step * second_b).astype(BF16)
-
-    def power(rate_, span, count):
-        return jnp.exp(-rate_ * (float(span) * jnp.maximum(count, 0).astype(F32)))
 
     def total(buf, span, rate_):
         p1 = jnp.exp(-rate_ * float(span))
@@ -209,32 +204,32 @@
             sum_b = sum_b * p1 + buf[3 - j, 1].astype(F32)
         return sum_a, sum_b
 
-    def exclusive(buf, span, place, rate_, before, after):
-        sum_a = before * power(rate_, span, place)
-        sum_b = after * power(rate_, span, 3 - place)
+    def exclusive(buf, span, rate_, before, after, dst):
+        p1 = jnp.exp(-rate_ * float(span))
         for j in range(4):
-            sum_a += (j < place).astype(F32) * power(rate_, span, place - 1 - j) * buf[j, 0].astype(F32)
-            sum_b += (j > place).astype(F32) * power(rate_, span, j - 1 - place) * buf[j, 1].astype(F32)
-        return sum_a, sum_b
+            dst[j, 0], dst[3 - j, 1] = before.astype(BF16), after.astype(BF16)
+            if j < 3:
+                before = before * p1 + buf[j, 0].astype(F32)
+                after = after * p1 + buf[3 - j, 1].astype(F32)
 
     def put(ref, pair):
         ref[0], ref[1] = pair[0].astype(BF16), pair[1].astype(BF16)
 
     copies = []
     for k, d in enumerate((1, 2, 3)):
-        piece = send_x.at[:, :, lanes_of(((px + d) % 4) * quarter, quarter)]
-        copies.append(push(piece, buf_x.at[px], sem_x, k, mates_x[k]))
+        part = send_x.at[:, :, lanes_of(((px + d) % 4) * quarter, quarter)]
+        copies.append(push(part, buf_x.at[px], sem_x, k, mates_x[k]))
     buf_x[px] = send_x[:, :, lanes_of(px * quarter, quarter)]
     rate_x = rate_lanes[:, lanes_of(c * half + px * quarter, quarter)]
     rate_y = rate_lanes[:, lanes_of(c * half + px * quarter + py * eighth, eighth)]
-    local_pieces(1, 4)
+    local_pieces(2, 4)
     for copy in copies:
         copy.wait()
     put(send_y, total(buf_x, 256, rate_x))
     copies = []
     for k, d in enumerate((1, 2, 3)):
-        piece = send_y.at[:, :, lanes_of(((py + d) % 4) * eighth, eighth)]
-        copies.append(push(piece, buf_y.at[py], sem_y, k, mates_y[k]))
+        part = send_y.at[:, :, lanes_of(((py + d) % 4) * eighth, eighth)]
+        copies.append(push(part, buf_y.at[py], sem_y, k, mates_y[k]))
     buf_y[py] = send_y[:, :, lanes_of(py * eighth, eighth)]
     push_halo(0, 3)
     local_pieces(4, 6)
@@ -247,26 +242,25 @@
     for copy in copies:
         copy.wait()
     zero = jnp.zeros_like(rate_y)
-    before, after = exclusive(buf_z, 4096, pz, rate_y, zero, zero)
+    exclusive(buf_z, 4096, rate_y, zero, zero, push_z)
+    exclusive(buf_y, 1024, rate_y, push_z[pz, 0].astype(F32), push_z[pz, 1].astype(F32), push_y)
     copies = []
     for k, d in enumerate((1, 2, 3)):
-        put(push_y.at[k], exclusive(buf_y, 1024, (py + d) % 4, rate_y, before, after))
-        copies.append(push(push_y.at[k], buf_w.at[py], sem_w, k, mates_y[k]))
-    put(buf_w.at[py], exclusive(buf_y, 1024, py, rate_y, before, after))
+        copies.append(push(push_y.at[(py + d) % 4], buf_w.at[py], sem_w, k, mates_y[k]))
+    buf_w[py] = push_y[py]
     over_blocks(medium_tables, 0, blocks // 2)
     for copy in copies:
         copy.wait()
     before = jnp.concatenate([buf_w[j, 0] for j in range(4)], axis=1).astype(F32)
     after = jnp.concatenate([buf_w[j, 1] for j in range(4)], axis=1).astype(F32)
+    exclusive(buf_x, 256, rate_x, before, after, push_x)
     copies = []
     for k, d in enumerate((1, 2, 3)):
-        put(push_x.at[k], exclusive(buf_x, 256, (px + d) % 4, rate_x, before, after))
-        copies.append(push(push_x.at[k], buf_r.at[px], sem_r, k, mates_x[k]))
-    put(buf_r.at[px], exclusive(buf_x, 256, px, rate_x, before, after))
+        copies.append(push(push_x.at[(px + d) % 4], buf_r.at[px], sem_r, k, mates_x[k]))
+    buf_r[px] = push_x[px]
     over_blocks(medium_tables, blocks // 2, blocks // 2)
     for copy in copies:
         copy.wait()
-    push_halo(3, SPLIT)
     for j in range(4):
         lanes = pl.ds(j * quarter, quarter)
         part = slice(j * quarter, (j + 1) * quarter)
@@ -279,6 +273,8 @@
         states[0, :, keep] = jnp.where(c == 0, early_a, late_a).astype(BF16)
         states[1, :, keep] = jnp.where(c == 0, early_b, late_b).astype(BF16)
     push(push_c, states.at[:, :, mine], sem_d, 0, partner).wait()
+    near_copy = push(states.at[1], near, sem_n, 0, previous)
+    push_halo(3, SPLIT)
 
     for u in range(UNROLL):
         rows[u, L : L + 8, :] = jnp.zeros((8, L), F32)
@@ -289,8 +285,8 @@
     def adjoint_filters(b, u):
         cols = lanes_of(b * L, L)
         into = (weight[pl.ds(b, 1), :] * jnp.exp(-rate[pl.ds(b, 1), :] * (L - sub).astype(F32))).astype(BF16)
-        far = states[1, :, cols].astype(F32)
-        close = near[:, cols].astype(F32) + jnp.exp(-rate_lanes[:, cols] * 128.0) * far
+        close = states[1, :, cols].astype(F32)
+        far = jnp.where(last, 0.0, near[:, cols].astype(F32))
         entering = spread_groups(jnp.concatenate([close, far], axis=1)).astype(BF16)
         beyond = jnp.where(last, 0.0, halo[:, cols].astype(F32))
         inside = jnp.concatenate([adj[:, cols].astype(F32), beyond], axis=1)
@@ -317,16 +313,27 @@
         gate_out[:, cols] = (og[:, cols].astype(F32) * full.astype(F32)).astype(BF16)
 
     head_copies, stores = [], []
+
+    def store(src, dst, sem):
+        stores.append(pltpu.make_async_copy(src, dst, sem))
+        stores[-1].start()
+
+    def gate_pieces(first, stop):
+        for k in range(first, stop):
+            cols = slice(k * wide, (k + 1) * wide)
+            over_blocks(gate_gradient, k * size, size)
+            store(gate_out.at[:, cols], gate_done.at[:, cols], sem_o.at[0, k])
+
+    gate_pieces(0, 6)
+    near_copy.wait()
     for k in range(SPLIT):
-        cols = slice(k * wide, (k + 1) * wide)
+        start = piece(k, 1 - c)
+        cols = lanes_of(start * wide, wide)
         halo_copies[k].wait()
-        over_blocks(adjoint_filters, k * size, size)
+        over_blocks(adjoint_filters, start * size, size)
         head_copies.append(push(head.at[:, cols], head_next.at[:, cols], sem_e, k, previous))
-        over_blocks(gate_gradient, k * size, size)
-        stores.append(pltpu.make_async_copy(gate_out.at[:, cols], gate_done.at[:, cols], sem_o.at[0, k]))
-        stores.append(pltpu.make_async_copy(grad_out.at[0:112, cols], grad_done.at[0:112, cols], sem_o.at[1, k]))
-        for copy in stores[-2:]:
-            copy.start()
+        store(grad_out.at[0:112, cols], grad_done.at[0:112, cols], sem_o.at[1, k])
+    gate_pieces(6, SPLIT)
     for copy in head_copies:
         copy.wait()
 
@@ -371,8 +378,6 @@
             vmem((7, channels), BF16),
             vmem((groups, L), F32),
             wide,
-            wide,
-            vmem((groups, L), F32),
             vmem((16, channels), F32),
             vmem((2, 16, channels), BF16),
             vmem((16, channels), BF16),
@@ -386,9 +391,10 @@
             vmem((4, 2, 16, eighth), BF16),
             vmem((2, 16, eighth), BF16),
             vmem((4, 2, 16, eighth), BF16),
-            vmem((3, 2, 16, eighth), BF16),
             vmem((4, 2, 16, eighth), BF16),
-            vmem((3, 2, 16, quarter), BF16),
+            vmem((4, 2, 16, eighth), BF16),
+            vmem((4, 2, 16, eighth), BF16),
+            vmem((4, 2, 16, quarter), BF16),
             vmem((4, 2, 16, quarter), BF16),
             vmem((2, 16, half), BF16),
             vmem((2, 16, channels), BF16),
@@ -397,7 +403,7 @@
             vmem((16, channels), F32),
             vmem((UNROLL, L + 8, L), F32),
             vmem((UNROLL, 24, L), F32),
-            dma((3,)), dma((3, SPLIT)), dma((2, 5)), dma((5,)), dma((2, 1)), dma((2, 2)), dma((2, 3)), dma((2, 3)), dma((2, 3)),
+            dma((3,)), dma((3, SPLIT)), dma((2, 5)), dma((5,)), dma((2, 1)), dma((2, 1)), dma((2, 3)), dma((2, 3)), dma((2, 3)),
             dma((2, 3)), dma((2, 3)), dma((2, 1)), dma((2, SPLIT)), dma((2, SPLIT)),
         ],
         compiler_params=pltpu.CompilerParams(

time: 84.8 us -> 80.9 us (0.954)
  Pallas kernels: 79.5 us -> 75.5 us
    pallas_call x1, Pallas kernels: 79.5 us -> 75.5 us  [on_device(): pl.pallas_call(kernel, out_shape=(jax.ShapeDtypeStruct(x.shape, BF16),) *...]
where the time goes in v2:
time: 80.9 us; the launch traced here: 80.7 us
  Pallas kernels  75.5 us (93%)
  local copies, waits for them, and re-layouts  4.57 us (6%)
    pallas_call x1, Pallas kernels, on_device(): pl.pallas_call(kernel, out_shape=(jax.ShapeDtypeStruct(x.shape, BF16),) *...  75.5 us
    unnamed x4, local copies, waits for them, and re-layouts  4.57 us

profile of v2, /device:TPU:31, one launch (start us, length us, event | category | flops | bytes accessed | tf_op | source)
XLA Modules:
  0.0 80.7 jit_solution(11614130448757873468)
XLA Ops:
  0.6 75.5 %shard_map.95 = (bf16[128,8192]{1,0:T(8,128)(2,1)}, bf16[128,8192]{1,0:T(8,128)(2,1)}) custom-call(bf16[128,8192]{1,0:T(8,128)(2,1)} %x_in.1, bf16[128,8192]{1,0:T(8,128)(2,1)} %gate_in.1, bf16[128,8192]{1,0:T(8,128)(2,1)} %og_in.1, f32[16,256]{1,0:T(8,128)} %bitcast.3, f32[16,256]{1,0:T(8,128)} %bitcast.4, f32[32,128]{1,0:T(8,128)} %bitcast.5, ...), custom_call_target="tpu_custom_call" | custom-call | tf_op jit(solution)/shard_map/pallas_call | solution.py:364
  76.2 0.0 copy-start
  76.2 3.2 %copy.12 = bf16[128,8192]{1,0:T(8,128)(2,1)} copy(bf16[128,8192]{1,0:T(8,128)(2,1)} %get-tuple-element.4) | data formatting | bytes 4194304
  79.4 0.0 copy-done
  79.4 1.3 %copy.13 = bf16[128,8192]{1,0:T(8,128)(2,1)} copy(bf16[128,8192]{1,0:T(8,128)(2,1)S(1)} %copy-done) | data formatting | bytes 4194304
Async XLA Ops:
  76.2 3.3 %copy-start = (bf16[128,8192]{1,0:T(8,128)(2,1)S(1)}, bf16[128,8192]{1,0:T(8,128)(2,1)}, u32[]{:S(2)}) copy-start(bf16[128,8192]{1,0:T(8,128)(2,1)} %get-tuple-element.5) | copy-start | bytes 6291460

commit v3 on v2

--- a/solution.py
+++ b/solution.py
@@ -53,14 +53,14 @@
     x_in, gate_in, og_in, rate_in, weight_in, direct_in, short_in, medium_in, grad_done, gate_done,
     x, gate, og, grad_out, gate_out, rate_by_group, weight_by_group, medium_raw, circ,
     rate, weight, direct, short, medium, grad_y, rate_lanes, sums, near, conv, adj, halo,
-    buf_c, send_x, buf_x, send_y, buf_y, send_z, buf_z, push_z, push_y, buf_w, push_x, buf_r, push_c, states,
+    buf_c, send_x, buf_x, send_y, buf_y, push_y, buf_w, push_x, buf_r, push_c, states,
     head, head_next, tail, rows, ends,
-    sem_i, sem_o, sem_p, sem_l, sem_n, sem_c, sem_x, sem_y, sem_z, sem_w, sem_r, sem_d, sem_h, sem_e,
+    sem_i, sem_o, sem_p, sem_l, sem_n, sem_c, sem_x, sem_y, sem_w, sem_r, sem_d, sem_h, sem_e,
 ):
     channels = x_in.shape[1]
     blocks = channels // L
     wide = channels // SPLIT
-    half, quarter, eighth = channels // 2, channels // 8, channels // 32
+    half, quarter = channels // 2, channels // 8
     ctx, c = lax.axis_index("ctx"), lax.axis_index("ch")
     px, py, pz = ctx % 4, (ctx // 4) % 4, ctx // 16
     me = ctx * 2 + c
@@ -74,14 +74,15 @@
     previous = (before_me // 2, before_me % 2)
     following = (after_me // 2, after_me % 2)
     mates_x = [at(pz, py, (px + d) % 4) for d in (1, 2, 3)]
-    mates_y = [at(pz, (py + d) % 4, px) for d in (1, 2, 3)]
-    mates_z = [at((pz + d) % 4, py, px) for d in (1, 2, 3)]
+    row = pz * 4 + py
+    others = [(row + d) % 16 for d in range(1, 16)]
+    mates_row = [at(other // 4, other % 4, px) for other in others]
     loads = []
     for k, (src, dst) in enumerate([(x_in, x), (gate_in, gate), (og_in, og)]):
         loads.append(pltpu.make_async_copy(src, dst, sem_i.at[k]))
         loads[-1].start()
     barrier = pltpu.get_barrier_semaphore()
-    for mate in [partner, following] + mates_x + mates_y + mates_z:
+    for mate in [partner, following] + mates_x + mates_row:
         pl.semaphore_signal(barrier, inc=1, device_id=mate, device_id_type=MESH)
 
     def push(src, dst, sem, k, mate):
@@ -176,9 +177,10 @@
             halo_copies.append(push(adj.at[:, cols], halo.at[:, cols], sem_h, k, previous))
 
     over_blocks(block_sums, c * (blocks // 2), blocks // 2)
-    pl.semaphore_wait(barrier, 11)
+    pl.semaphore_wait(barrier, 20)
     gathers = [push(own, place, sem_p, k, partner) for k, (own, place) in enumerate(places)]
     local_pieces(0, 1)
+    push_halo(0, 1)
     for copy in gathers:
         copy.wait()
     over_blocks(block_sums, (1 - c) * (blocks // 2), blocks // 2)
@@ -221,38 +223,37 @@
         copies.append(push(part, buf_x.at[px], sem_x, k, mates_x[k]))
     buf_x[px] = send_x[:, :, lanes_of(px * quarter, quarter)]
     rate_x = rate_lanes[:, lanes_of(c * half + px * quarter, quarter)]
-    rate_y = rate_lanes[:, lanes_of(c * half + px * quarter + py * eighth, eighth)]
+    rate_row = rate_lanes[:, lanes_of(c * half + px * quarter + (row % 8) * L, L)]
     local_pieces(2, 4)
     for copy in copies:
         copy.wait()
     put(send_y, total(buf_x, 256, rate_x))
     copies = []
-    for k, d in enumerate((1, 2, 3)):
-        part = send_y.at[:, :, lanes_of(((py + d) % 4) * eighth, eighth)]
-        copies.append(push(part, buf_y.at[py], sem_y, k, mates_y[k]))
-    buf_y[py] = send_y[:, :, lanes_of(py * eighth, eighth)]
-    push_halo(0, 3)
-    local_pieces(4, 6)
+    for k, other in enumerate(others):
+        part = send_y.at[other // 8, :, lanes_of((other % 8) * L, L)]
+        copies.append(push(part, buf_y.at[row], sem_y, k, mates_row[k]))
+    buf_y[row] = send_y[row // 8, :, lanes_of((row % 8) * L, L)]
+    push_halo(1, 3)
+    local_pieces(4, 7)
     for copy in copies:
         copy.wait()
-    put(send_z, total(buf_y, 1024, rate_y))
-    copies = [push(send_z, buf_z.at[pz], sem_z, k, mates_z[k]) for k in range(3)]
-    buf_z[pz] = send_z[...]
-    local_pieces(6, 8)
-    for copy in copies:
-        copy.wait()
-    zero = jnp.zeros_like(rate_y)
-    exclusive(buf_z, 4096, rate_y, zero, zero, push_z)
-    exclusive(buf_y, 1024, rate_y, push_z[pz, 0].astype(F32), push_z[pz, 1].astype(F32), push_y)
+    p1 = jnp.exp(-rate_row * 1024.0)
+    state = jnp.zeros_like(rate_row)
+    for j in range(16):
+        place = jnp.where(row < 8, j, 15 - j)
+        push_y[place] = state.astype(BF16)
+        state = state * p1 + buf_y[place].astype(F32)
     copies = []
-    for k, d in enumerate((1, 2, 3)):
-        copies.append(push(push_y.at[(py + d) % 4], buf_w.at[py], sem_w, k, mates_y[k]))
-    buf_w[py] = push_y[py]
+    for k, other in enumerate(others):
+        copies.append(push(push_y.at[other], buf_w.at[row], sem_w, k, mates_row[k]))
+    buf_w[row] = push_y[row]
+    push_halo(3, 5)
+    local_pieces(7, SPLIT)
     over_blocks(medium_tables, 0, blocks // 2)
     for copy in copies:
         copy.wait()
-    before = jnp.concatenate([buf_w[j, 0] for j in range(4)], axis=1).astype(F32)
-    after = jnp.concatenate([buf_w[j, 1] for j in range(4)], axis=1).astype(F32)
+    before = jnp.concatenate([buf_w[j] for j in range(8)], axis=1).astype(F32)
+    after = jnp.concatenate([buf_w[j + 8] for j in range(8)], axis=1).astype(F32)
     exclusive(buf_x, 256, rate_x, before, after, push_x)
     copies = []
     for k, d in enumerate((1, 2, 3)):
@@ -274,7 +275,7 @@
         states[1, :, keep] = jnp.where(c == 0, early_b, late_b).astype(BF16)
     push(push_c, states.at[:, :, mine], sem_d, 0, partner).wait()
     near_copy = push(states.at[1], near, sem_n, 0, previous)
-    push_halo(3, SPLIT)
+    push_halo(5, SPLIT)
 
     for u in range(UNROLL):
         rows[u, L : L + 8, :] = jnp.zeros((8, L), F32)
@@ -358,7 +359,7 @@
     channels = x.shape[1]
     groups = channels // 16
     rows = decay_rates.shape[0] // G
-    half, quarter, eighth = channels // 2, channels // 8, channels // 32
+    half, quarter = channels // 2, channels // 8
     wide = pltpu.VMEM((L, channels), BF16)
     vmem, dma = pltpu.VMEM, pltpu.SemaphoreType.DMA
     return pl.pallas_call(
@@ -388,12 +389,9 @@
             vmem((2, 16, half), BF16),
             vmem((4, 2, 16, quarter), BF16),
             vmem((2, 16, quarter), BF16),
-            vmem((4, 2, 16, eighth), BF16),
-            vmem((2, 16, eighth), BF16),
-            vmem((4, 2, 16, eighth), BF16),
-            vmem((4, 2, 16, eighth), BF16),
-            vmem((4, 2, 16, eighth), BF16),
-            vmem((4, 2, 16, eighth), BF16),
+            vmem((16, 16, L), BF16),
+            vmem((16, 16, L), BF16),
+            vmem((16, 16, L), BF16),
             vmem((4, 2, 16, quarter), BF16),
             vmem((4, 2, 16, quarter), BF16),
             vmem((2, 16, half), BF16),
@@ -403,8 +401,8 @@
             vmem((16, channels), F32),
             vmem((UNROLL, L + 8, L), F32),
             vmem((UNROLL, 24, L), F32),
-            dma((3,)), dma((3, SPLIT)), dma((2, 5)), dma((5,)), dma((2, 1)), dma((2, 1)), dma((2, 3)), dma((2, 3)), dma((2, 3)),
-            dma((2, 3)), dma((2, 3)), dma((2, 1)), dma((2, SPLIT)), dma((2, SPLIT)),
+            dma((3,)), dma((3, SPLIT)), dma((2, 5)), dma((5,)), dma((2, 1)), dma((2, 1)), dma((2, 3)), dma((2, 15)),
+            dma((2, 15)), dma((2, 3)), dma((2, 1)), dma((2, SPLIT)), dma((2, SPLIT)),
         ],
         compiler_params=pltpu.CompilerParams(
             collective_id=0, has_side_effects=True, vmem_limit_bytes=58 * 2**20

time: 80.9 us -> 78.6 us (0.972)
  the two profiles are of different devices: /device:TPU:31 before, /device:TPU:7 now
where the time goes in v3:
time: 78.6 us; the launch traced here: 78.5 us
  Pallas kernels  73.2 us (93%)
  local copies, waits for them, and re-layouts  4.57 us (6%)
    pallas_call x1, Pallas kernels, on_device(): pl.pallas_call(kernel, out_shape=(jax.ShapeDtypeStruct(x.shape, BF16),) *...  73.2 us
    unnamed x4, local copies, waits for them, and re-layouts  4.57 us

profile of v3, /device:TPU:7, one launch (start us, length us, event | category | flops | bytes accessed | tf_op | source)
XLA Modules:
  0.0 78.5 jit_solution(6936936275350737875)
XLA Ops:
  0.6 73.2 %shard_map.95 = (bf16[128,8192]{1,0:T(8,128)(2,1)}, bf16[128,8192]{1,0:T(8,128)(2,1)}) custom-call(bf16[128,8192]{1,0:T(8,128)(2,1)} %x_in.1, bf16[128,8192]{1,0:T(8,128)(2,1)} %gate_in.1, bf16[128,8192]{1,0:T(8,128)(2,1)} %og_in.1, f32[16,256]{1,0:T(8,128)} %bitcast.3, f32[16,256]{1,0:T(8,128)} %bitcast.4, f32[32,128]{1,0:T(8,128)} %bitcast.5, ...), custom_call_target="tpu_custom_call" | custom-call | tf_op jit(solution)/shard_map/pallas_call | solution.py:365
  73.9 0.0 copy-start
  73.9 3.2 %copy.12 = bf16[128,8192]{1,0:T(8,128)(2,1)} copy(bf16[128,8192]{1,0:T(8,128)(2,1)} %get-tuple-element.4) | data formatting | bytes 4194304
  77.1 0.0 copy-done
  77.1 1.3 %copy.13 = bf16[128,8192]{1,0:T(8,128)(2,1)} copy(bf16[128,8192]{1,0:T(8,128)(2,1)S(1)} %copy-done) | data formatting | bytes 4194304
Async XLA Ops:
  73.9 3.3 %copy-start = (bf16[128,8192]{1,0:T(8,128)(2,1)S(1)}, bf16[128,8192]{1,0:T(8,128)(2,1)}, u32[]{:S(2)}) copy-start(bf16[128,8192]{1,0:T(8,128)(2,1)} %get-tuple-element.5) | copy-start | bytes 6291460

commit v4 on v3

--- a/solution.py
+++ b/solution.py
@@ -168,8 +168,7 @@
         return (core * (SPLIT // 2) + k) % SPLIT
 
     def local_pieces(first, stop):
-        for k in range(first, stop):
-            over_blocks(local_products, piece(k, c) * size, size)
+        over_blocks(local_products, piece(first, c) * size, (stop - first) * size)
 
     def push_halo(first, stop):
         for k in range(first, stop):
@@ -320,9 +319,9 @@
         stores[-1].start()
 
     def gate_pieces(first, stop):
+        over_blocks(gate_gradient, first * size, (stop - first) * size)
         for k in range(first, stop):
             cols = slice(k * wide, (k + 1) * wide)
-            over_blocks(gate_gradient, k * size, size)
             store(gate_out.at[:, cols], gate_done.at[:, cols], sem_o.at[0, k])
 
     gate_pieces(0, 6)

time: 78.6 us -> 78.6 us (level)
  no operation moved by 1% of the time
where the time goes in v4:
time: 78.6 us; the launch traced here: 78.5 us
  Pallas kernels  73.3 us (93%)
  local copies, waits for them, and re-layouts  4.57 us (6%)
    pallas_call x1, Pallas kernels, on_device(): pl.pallas_call(kernel, out_shape=(jax.ShapeDtypeStruct(x.shape, BF16),) *...  73.3 us
    unnamed x4, local copies, waits for them, and re-layouts  4.57 us

profile of v4, /device:TPU:7, one launch (start us, length us, event | category | flops | bytes accessed | tf_op | source)
XLA Modules:
  0.0 78.5 jit_solution(1902861467714600372)
XLA Ops:
  0.6 73.3 %shard_map.95 = (bf16[128,8192]{1,0:T(8,128)(2,1)}, bf16[128,8192]{1,0:T(8,128)(2,1)}) custom-call(bf16[128,8192]{1,0:T(8,128)(2,1)} %x_in.1, bf16[128,8192]{1,0:T(8,128)(2,1)} %gate_in.1, bf16[128,8192]{1,0:T(8,128)(2,1)} %og_in.1, f32[16,256]{1,0:T(8,128)} %bitcast.3, f32[16,256]{1,0:T(8,128)} %bitcast.4, f32[32,128]{1,0:T(8,128)} %bitcast.5, ...), custom_call_target="tpu_custom_call" | custom-call | tf_op jit(solution)/shard_map/pallas_call | solution.py:364
  73.9 0.0 copy-start
  73.9 3.2 %copy.12 = bf16[128,8192]{1,0:T(8,128)(2,1)} copy(bf16[128,8192]{1,0:T(8,128)(2,1)} %get-tuple-element.4) | data formatting | bytes 4194304
  77.2 0.0 copy-done
  77.2 1.3 %copy.13 = bf16[128,8192]{1,0:T(8,128)(2,1)} copy(bf16[128,8192]{1,0:T(8,128)(2,1)S(1)} %copy-done) | data formatting | bytes 4194304
Async XLA Ops:
  73.9 3.3 %copy-start = (bf16[128,8192]{1,0:T(8,128)(2,1)S(1)}, bf16[128,8192]{1,0:T(8,128)(2,1)}, u32[]{:S(2)}) copy-start(bf16[128,8192]{1,0:T(8,128)(2,1)} %get-tuple-element.5) | copy-start | bytes 6291460
